TPU v7x, 32 devices: a whole 2x2x4 slice. The times are simulated.
32 devices in a mesh: ctx: 8 (over z, core), exp: 4 (over y, x).
Axes of the slice: x: 2, y: 2, z: 4, core: 2. Of those that a mesh axis runs over, the one named last changes fastest.
Arguments:
- tokens: bfloat16 [16384, 1024], P(('ctx', 'exp')), may hold values from -30 to 30
- slot_keys: bfloat16 [1024, 512], replicated, may hold values from -64 to 64
- expert_in: bfloat16 [16, 1024, 2048], P('exp'), may hold values from -0.1875 to 0.1875
- expert_out: bfloat16 [16, 2048, 1024], P('exp'), may hold values from -0.25 to 0.25
- slot_counts: int32 [32, 16], P(('ctx', 'exp')), may hold values from 0 to 64, as said below
- slot_reach: int32 [32, 8], P(('ctx', 'exp')), may hold values from 0 to 7, as said below
Outputs:
- mixed: bfloat16 [16384, 1024], P(('ctx', 'exp'))
Inputs may be any that keep to these rules, and one draw needn't show every extreme that they name: `slot_counts`: row k gives, in expert order, how many of the 512 slots of window k each expert takes; every row sums to 512; one expert, the same in every row, takes exactly 64 slots in every row. `slot_reach`: entry [k, j] is the last token block read by slots j * 64 to (j + 1) * 64 - 1 of window k; every row holds a 0 and a 7.
All inputs are finite; a program needn't handle non-finite values.
Results may differ from a plain program's by a relative error of at most 0.012.
The roundings to bfloat16 on the way count: a program that leaves them out, or rounds other values in their place, can miss the bound.
Values may be sent and summed in bfloat16 or wider, within the bound.
A program may use at most 64 MiB of HBM per device.

v0:
```python
import jax
import jax.numpy as jnp
from jax import lax
from jax.sharding import PartitionSpec as P

BLOCK = 64


EPSILON = 1e-06


def passed_along(block, axis, distance):
    devices = range(lax.axis_size(axis))
    route = [(i - distance, i) for i in devices if i - distance in devices]
    return lax.ppermute(block, axis, route)


def normalize(values):
    floats = values.astype(jnp.float32)
    inverse_rms = lax.rsqrt(jnp.mean(floats * floats, axis=-1, keepdims=True) + EPSILON)
    return (floats * inverse_rms).astype(jnp.bfloat16)


def block_levels(reach_row, slot_count):
    block_count = reach_row.shape[0]
    block_width = slot_count // block_count
    return jnp.broadcast_to(reach_row[:, None], (block_count, block_width)).reshape(slot_count)


def token_levels(tok_count):
    return jnp.arange(tok_count, dtype=jnp.int32) // BLOCK


def slot_layout(counts_row, slot_count, capacity):
    expert_count = counts_row.shape[0]
    expert_ids = jnp.arange(expert_count, dtype=jnp.int32)
    slot_ends = jnp.cumsum(counts_row)
    starts = slot_ends - counts_row
    slot_ids = jnp.arange(slot_count, dtype=jnp.int32)
    owner_ids = jnp.sum((slot_ends[None, :] <= slot_ids[:, None]).astype(jnp.int32), axis=1)
    onehot = owner_ids[:, None] == expert_ids[None, :]
    first_slot = jnp.sum(jnp.where(onehot, starts[None, :], 0), axis=1)
    padded_index = owner_ids * capacity + slot_ids - first_slot
    place_ids = jnp.arange(expert_count * capacity, dtype=jnp.int32)
    expert_of = place_ids // capacity
    position = place_ids - expert_of * capacity
    place_hot = expert_of[:, None] == expert_ids[None, :]
    counts_of = jnp.sum(jnp.where(place_hot, counts_row[None, :], 0), axis=1)
    starts_of = jnp.sum(jnp.where(place_hot, starts[None, :], 0), axis=1)
    is_live = position < counts_of
    source = jnp.clip(starts_of + position, 0, slot_count - 1)
    return (padded_index, is_live, source)


def dispatch_window(normed, slot_keys, reach_row, counts_row):
    tok_count = normed.shape[0]
    slot_count = slot_keys.shape[1]
    capacity = 2 * slot_count // counts_row.shape[0]
    logits = jnp.dot(normed, slot_keys, preferred_element_type=jnp.float32)
    allowed = token_levels(tok_count)[:, None] <= block_levels(reach_row, slot_count)[None, :]
    masked = jnp.where(allowed, logits, -jnp.inf)
    exponent = jnp.exp(masked - jnp.max(masked, axis=0, keepdims=True))
    weights = (exponent / jnp.sum(exponent, axis=0, keepdims=True)).astype(jnp.bfloat16)
    slot_inputs = lax.dot_general(
        weights, normed, (((0,), (0,)), ((), ())), preferred_element_type=jnp.float32
    ).astype(jnp.bfloat16)
    padded_index, is_live, source = slot_layout(counts_row, slot_count, capacity)
    packed = jnp.where(
        is_live[:, None], jnp.take(slot_inputs, source, axis=0), jnp.zeros((), jnp.bfloat16)
    )
    return (logits, packed, padded_index)


def combine_window(logits, reach_row, own_out, prior_out, has_prior):
    tok_count, slot_count = logits.shape
    allowed = block_levels(reach_row, slot_count)[None, :] <= token_levels(tok_count)[:, None]
    usable = jnp.logical_or(allowed, has_prior)
    largest = jnp.max(jnp.where(usable, logits, -jnp.inf), axis=1, keepdims=True)
    own_exp = jnp.exp(jnp.where(allowed, logits, -jnp.inf) - largest)
    prior_exp = jnp.exp(jnp.where(has_prior, logits, -jnp.inf) - largest)
    denominator = jnp.sum(own_exp + prior_exp, axis=1, keepdims=True)
    own_weights = (own_exp / denominator).astype(jnp.bfloat16)
    prior_weights = (prior_exp / denominator).astype(jnp.bfloat16)
    summed = jnp.dot(own_weights, own_out, preferred_element_type=jnp.float32)
    summed = summed + jnp.dot(prior_weights, prior_out, preferred_element_type=jnp.float32)
    return summed.astype(jnp.bfloat16)


def local_experts(received, w_first, w_second):
    hidden = jnp.einsum("epcd,edh->epch", received, w_first, preferred_element_type=jnp.float32)
    hidden = jax.nn.gelu(hidden, approximate=True).astype(jnp.bfloat16)
    return jnp.einsum(
        "epch,ehd->epcd", hidden, w_second, preferred_element_type=jnp.float32
    ).astype(jnp.bfloat16)


def local(tokens, slot_keys, expert_in, expert_out, slot_counts, slot_reach):
    normed = normalize(tokens)
    logits, packed, padded_index = dispatch_window(normed, slot_keys, slot_reach[0], slot_counts[0])
    experts = slot_counts.shape[1]
    model_width = tokens.shape[1]
    outgoing = packed.reshape(experts, 1, -1, model_width)
    received = lax.all_to_all(outgoing, "exp", split_axis=0, concat_axis=1, tiled=True)
    produced = local_experts(received, expert_in, expert_out)
    returned = lax.all_to_all(produced, "exp", split_axis=1, concat_axis=0, tiled=True)
    own_out = jnp.take(returned.reshape(-1, model_width), padded_index, axis=0)
    prior_out = passed_along(own_out, ("ctx", "exp"), 1)
    window_id = lax.axis_index("ctx") * lax.axis_size("exp") + lax.axis_index("exp")
    return combine_window(logits, slot_reach[0], own_out, prior_out, window_id > 0)


def solution(mesh):
    placed = (
        P(("ctx", "exp"), None),
        P(),
        P("exp", None, None),
        P("exp", None, None),
        P(("ctx", "exp"), None),
        P(("ctx", "exp"), None),
    )
    return jax.shard_map(
        local, mesh=mesh, in_specs=placed, out_specs=P(("ctx", "exp"), None), check_vma=False
    )
```

profile of v0, /device:TPU:25, one launch (start us, length us, event | category | flops | bytes accessed | tf_op | source)
XLA Modules:
  0.0 123.9 jit_solution(3342114166609513374)
XLA Ops:
  0.0 0.0 copy-start
  0.0 0.8 broadcast_in_dim.101
  0.8 0.1 le.62
  0.9 1.5 %fusion.14 = f32[512]{0:T(512)S(1)} fusion(bf16[512,1024]{1,0:T(8,128)(2,1)} %param.6), kind=kLoop, calls=%fused_computation.17 | loop fusion | flops 1572352 | bytes 1050624 | tf_op jit(solution)/shard_map/reduce_sum | solution.py:20
  2.4 0.0 copy-done
  2.4 0.0 copy-start.1
  2.5 2.3 %select_reduce_fusion = (f32[512]{0:T(512)S(1)}, f32[512]{0:T(512)S(1)}, f32[512,512]{1,0:T(8,128)S(1)}) fusion(s32[512]{0:T(512)S(1)} %le.62, s32[512]{0:T(512)S(1)} %add_select_fusion.2, pred[]{:T(512)S(6)} %gt.3, bf16[1024,512]{1,0:T(8,128)(2,1)S(1)} %copy-done, bf16[512,1024]{1,0:T(8,128)(2,1)} %param.6, f32[512]{0:T(512)S(1)} %add_rsqrt_fusion), kind=kOutput, calls=%fused_computation.35 | convolution fusion | flops 540277760 | bytes 3155969 | tf_op jit(solution)/shard_map/dot_general | solution.py:59
  4.7 0.0 copy-start.3
  4.7 0.8 add_reduce_fusion
  5.5 0.0 copy-done.1
  5.6 0.0 copy-start.2
  5.6 0.9 convolution_convert_fusion
  6.5 0.0 copy-done.3
  6.5 0.0 copy-done.2
  6.5 0.1 copy.15
  6.6 0.1 reduce
  6.8 0.1 select_reduce_fusion.2
  6.9 0.1 reduce_sum.78
  7.0 0.1 reduce_sum.76
  7.0 5.4 %gather_fusion = bf16[1024,1024]{1,0:T(8,128)(2,1)} fusion(bf16[512,1024]{1,0:T(8,128)(2,1)S(1)} %convolution_convert_fusion, s32[1024]{0:T(1024)S(1)} %broadcast_clamp_fusion), kind=kCustom, calls=%fused_computation | custom fusion | bytes 4198400 | tf_op jit(solution)/shard_map/jit(_take)/gather | solution.py:69
  12.4 1.8 %select_select_fusion = bf16[16,1,64,1024]{3,2,1,0:T(8,128)(2,1)S(1)} fusion(bf16[16,1,64,1024]{3,2,1,0:T(8,128)(2,1)} %bitcast.47, pred[16,64]{1,0:T(8,128)(4,1)S(1)} %get-tuple-element.12, pred[16,64]{1,0:T(8,128)(4,1)S(1)} %get-tuple-element.13), kind=kLoop, calls=%fused_computation.22 | loop fusion | flops 2097152 | bytes 4196352 | tf_op jit(solution)/shard_map/jit(_where)/select_n | solution.py:68
  14.2 27.4 %all_to_all.33 = bf16[16,1,64,1024]{3,2,1,0:T(8,128)(2,1)S(1)} all-to-all(bf16[16,1,64,1024]{3,2,1,0:T(8,128)(2,1)S(1)} %select_select_fusion), channel_id=1, replica_groups=mesh['ctx'=8,'exp'=4] {'exp'}, dimensions={0} | all-to-all | bytes 4194304 | tf_op jit(solution)/shard_map/all_to_all | solution.py:103
  41.6 10.0 %fusion.11 = bf16[4,4,64,2048]{3,2,1,0:T(8,128)(2,1)S(1)} fusion(bf16[4,1024,2048]{2,1,0:T(8,128)(2,1)} %param.8, bf16[4,4,1,64,1024]{4,3,1,0,2:T(8,128)(2,1)S(1)} %bitcast.48), kind=kOutput, calls=%fused_computation.14 | convolution fusion | flops 4313841664 | bytes 23068672 | tf_op jit(solution)/shard_map/epcd,edh->epch/dot_general | solution.py:90
  51.6 8.4 %fusion.18 = bf16[4,4,64,1024]{3,2,1,0:T(8,128)(2,1)S(1)} fusion(bf16[4,4,64,2048]{3,2,1,0:T(8,128)(2,1)S(1)} %fusion.11, bf16[4,2048,1024]{2,1,0:T(8,128)(2,1)} %param.9), kind=kOutput, calls=%fused_computation.23 | convolution fusion | flops 4296015872 | bytes 23068672 | tf_op jit(solution)/shard_map/epch,ehd->epcd/dot_general | solution.py:92
  60.1 1.5 %copy.18 = bf16[4,4,64,1024]{3,2,0,1:T(8,128)(2,1)} copy(bf16[4,4,64,1024]{3,2,1,0:T(8,128)(2,1)S(1)} %fusion.18) | data formatting | bytes 4194304 | tf_op jit(solution)/shard_map/convert_element_type | solution.py:94
  61.6 3.6 %all-to-all-start.1 = ((bf16[4,4,64,1024]{3,2,0,1:T(8,128)(2,1)}), bf16[4,4,64,1024]{3,2,0,1:T(8,128)(2,1)S(1)}, u32[]{:S(2)}, u32[]{:S(2)}) async-start(bf16[4,4,64,1024]{3,2,0,1:T(8,128)(2,1)} %copy.18), calls=%async_computation.1 | async-start | bytes 4194304 | tf_op jit(solution)/shard_map/all_to_all | solution.py:105
  65.2 0.1 convert_reduce_fusion
  65.3 0.1 select_reduce_fusion.3
  65.4 24.1 %all-to-all-done.1 = bf16[4,4,64,1024]{3,2,0,1:T(8,128)(2,1)S(1)} async-done(((bf16[4,4,64,1024]{3,2,0,1:T(8,128)(2,1)}), bf16[4,4,64,1024]{3,2,0,1:T(8,128)(2,1)S(1)}, u32[]{:S(2)}, u32[]{:S(2)}) %all-to-all-start.1) | async-done | bytes 2097184 | tf_op jit(solution)/shard_map/all_to_all | solution.py:105
  89.6 2.8 %gather_fusion.1 = bf16[512,1024]{1,0:T(8,128)(2,1)} fusion(bf16[1024,1024]{1,0:T(8,128)(2,1)S(1)} %bitcast.46, s32[1024]{0:T(1024)S(1)} %pad_clamp_fusion), kind=kCustom, calls=%fused_computation.1 | custom fusion | bytes 2099200 | tf_op jit(solution)/shard_map/jit(_take)/gather | solution.py:106
  92.3 0.0 copy-start.4
  92.3 1.5 %broadcast_select_fusion = bf16[512,1024]{1,0:T(8,128)(2,1)S(1)} fusion(bf16[512,1024]{1,0:T(8,128)(2,1)} %gather_fusion.1, pred[512]{0:T(512)(128)(4,1)S(1)} %compare_and_fusion.1), kind=kLoop, calls=%fused_computation.36 | loop fusion | flops 524288 | bytes 2097664 | tf_op jit(solution)/shard_map/jit(_take)/select_n | solution.py:106
  93.8 1.9 %collective-permute-start = (bf16[512,1024]{1,0:T(8,128)(2,1)S(1)}, bf16[512,1024]{1,0:T(8,128)(2,1)S(1)}, u32[]{:S(2)}, u32[]{:S(2)}) collective-permute-start(bf16[512,1024]{1,0:T(8,128)(2,1)S(1)} %broadcast_select_fusion), channel_id=1, source_target_pairs={{0,1},{1,2},{2,3},{3,4},{4,5},{5,6},{6,7},{7,8},{8,9},{9,10},{10,1... | collective-permute-start | bytes 3145736 | tf_op jit(solution)/shard_map/ppermute | solution.py:15
  95.7 0.0 copy-done.4
  95.7 0.9 fusion.25
  96.6 25.4 %collective-permute-done = bf16[512,1024]{1,0:T(8,128)(2,1)S(1)} collective-permute-done((bf16[512,1024]{1,0:T(8,128)(2,1)S(1)}, bf16[512,1024]{1,0:T(8,128)(2,1)S(1)}, u32[]{:S(2)}, u32[]{:S(2)}) %collective-permute-start) | collective-permute-done | bytes 1048608 | tf_op jit(solution)/shard_map/ppermute | solution.py:15
  122.1 1.8 %add_convert_fusion = bf16[512,1024]{1,0:T(8,128)(2,1)} fusion(f32[512,1024]{1,0:T(8,128)S(1)} %fusion.25, bf16[512,1024]{1,0:T(8,128)(2,1)S(1)} %collective-permute-done, f32[512,512]{1,0:T(8,128)S(1)} %copy-done.4, f32[512]{0:T(512)S(1)} %get-tuple-element.5, f32[512]{0:T(512)S(1)} %get-tuple-element.7, pred[]{:T(512)S(6)} %gt.3), kind=kOutput, calls=%fused_computation.21 | convolution fusion | flops 538968064 | bytes 5246977 | tf_op jit(solution)/shard_map/dot_general | solution.py:85
  (12 shorter events, 0.1 us)
Async XLA Ops:
  0.0 2.4 %copy-start = (bf16[1024,512]{1,0:T(8,128)(2,1)S(1)}, bf16[1024,512]{1,0:T(8,128)(2,1)}, u32[]{:S(2)}) copy-start(bf16[1024,512]{1,0:T(8,128)(2,1)} %param.7) | copy-start | bytes 3145732
  2.4 3.1 %copy-start.1 = (bf16[512,1024]{1,0:T(8,128)(2,1)S(1)}, bf16[512,1024]{1,0:T(8,128)(2,1)}, u32[]{:S(2)}) copy-start(bf16[512,1024]{1,0:T(8,128)(2,1)} %param.6) | copy-start | bytes 3145732
  4.7 1.8 %copy-start.3 = (f32[512,512]{1,0:T(8,128)}, f32[512,512]{1,0:T(8,128)S(1)}, u32[]{:S(2)}) copy-start(f32[512,512]{1,0:T(8,128)S(1)} %get-tuple-element.11) | copy-start | bytes 3145732
  5.6 1.0 copy-start.2
  61.6 28.0 %all-to-all-start.1 = ((bf16[4,4,64,1024]{3,2,0,1:T(8,128)(2,1)}), bf16[4,4,64,1024]{3,2,0,1:T(8,128)(2,1)S(1)}, u32[]{:S(2)}, u32[]{:S(2)}) async-start(bf16[4,4,64,1024]{3,2,0,1:T(8,128)(2,1)} %copy.18), calls=%async_computation.1 | async-start | bytes 4194304 | tf_op jit(solution)/shard_map/all_to_all | solution.py:105
  92.3 3.4 %copy-start.4 = (f32[512,512]{1,0:T(8,128)S(1)}, f32[512,512]{1,0:T(8,128)}, u32[]{:S(2)}) copy-start(f32[512,512]{1,0:T(8,128)} %copy-done.3) | copy-start | bytes 3145732
  93.8 28.3 %collective-permute-start = (bf16[512,1024]{1,0:T(8,128)(2,1)S(1)}, bf16[512,1024]{1,0:T(8,128)(2,1)S(1)}, u32[]{:S(2)}, u32[]{:S(2)}) collective-permute-start(bf16[512,1024]{1,0:T(8,128)(2,1)S(1)} %broadcast_select_fusion), channel_id=1, source_target_pairs={{0,1},{1,2},{2,3},{3,4},{4,5},{5,6},{6,7},{7,8},{8,9},{9,10},{10,1... | collective-permute-start | bytes 3145736 | tf_op jit(solution)/shard_map/ppermute | solution.py:15
where the time goes:
time: 124 us
  waiting for transfers between devices  49.6 us (40%)
  blocking collectives  27.4 us (22%)
  matrix products  24.3 us (20%)
  local copies, waits for them, and re-layouts  10.8 us (9%)
  other arithmetic  6.09 us (5%)
  starting transfers between devices  5.53 us (4%)
    all_to_all x1, blocking collectives, local(): lax.all_to_all(outgoing, 'exp', split_axis=0, concat_axis=1, tiled=True)  27.4 us
    ppermute x1, waiting for transfers between devices, passed_along(): return lax.ppermute(block, axis, route)  25.4 us
    all_to_all x1, waiting for transfers between devices, local(): lax.all_to_all(produced, 'exp', split_axis=1, concat_axis=0, tiled=True)  24.1 us
    dot_general x1, matrix products, local_experts(): jnp.einsum('epcd,edh->epch', received, w_first, preferred_element_type=jn...  10 us
    dot_general x1, matrix products, local_experts(): jnp.einsum('epch,ehd->epcd', hidden, w_second, preferred_element_type=jnp...  8.41 us
    gather x1, local copies, waits for them, and re-layouts, dispatch_window(): jnp.take(slot_inputs, source, axis=0)  5.35 us
    all_to_all x1, starting transfers between devices, local(): lax.all_to_all(produced, 'exp', split_axis=1, concat_axis=0, tiled=True)  3.61 us
    gather x1, local copies, waits for them, and re-layouts, local(): own_out = jnp.take(returned.reshape(-1, model_width), padded_index, axis=0)  2.77 us
  transfers between devices with their start and end apart: 2, of which 2 were waited for; matrix products, arithmetic and copies ran while one was open for 1% of the time, Pallas kernels for 0%

commit v1 on v0

v1 whole, which is shorter than its diff:
```python
import functools

import jax
import jax.numpy as jnp
from jax import lax
from jax.experimental import pallas as pl
from jax.experimental.pallas import tpu as pltpu
from jax.sharding import PartitionSpec as P

BLOCK = 64
EPSILON = 1e-06
MESH = pl.DeviceIdType.MESH
ROWS = 64
PIECES = 4


def iota(shape, dim):
    return lax.broadcasted_iota(jnp.int32, shape, dim)


def dot(a, b):
    return jnp.dot(a, b, preferred_element_type=jnp.float32)


def pick(axis_ids, width, values):
    chosen = jnp.full(axis_ids.shape, values[0], jnp.int32)
    for i in range(1, len(values)):
        chosen = jnp.where(axis_ids >= i * width, values[i], chosen)
    return chosen


def kernel(
    n_ctx, n_exp, counts, reach, tokens, keys, first, second, out,
    first_v, second_v, normed, logits, weights, slot_in, send, recv, prod, ret, place, mix_w, mix_v,
    weight_sem, send_in, recv_in, send_out, recv_out, send_prior, recv_prior,
):
    toks, width = tokens.shape
    slots = keys.shape[1]
    local = first.shape[0]
    hidden = first.shape[2]
    experts = counts.shape[1]
    cap = 2 * slots // experts
    reach_width = slots // reach.shape[1]
    ctx, me = lax.axis_index("ctx"), lax.axis_index("exp")
    window = ctx * n_exp + me
    windows = n_ctx * n_exp
    after = lax.rem(window + 1, windows)
    before = lax.rem(window + windows - 1, windows)

    loads = []
    for j in range(local):
        for source, target, n in ((first, first_v, 0), (second, second_v, 1)):
            load = pltpu.make_async_copy(source.at[j], target.at[j], weight_sem.at[j, n])
            load.start()
            loads.append(load)

    barrier = pltpu.get_barrier_semaphore()
    for o in range(1, n_exp):
        pl.semaphore_signal(
            barrier, inc=1, device_id=(ctx, lax.rem(me + o, n_exp)), device_id_type=MESH
        )
    for other in (after, before):
        pl.semaphore_signal(
            barrier, inc=1, device_id=(other // n_exp, lax.rem(other, n_exp)), device_id_type=MESH
        )

    def normalize(i, carry):
        rows = pl.ds(pl.multiple_of(i * ROWS, ROWS), ROWS)
        floats = tokens[rows, :].astype(jnp.float32)
        scale = lax.rsqrt(jnp.mean(floats * floats, axis=-1, keepdims=True) + EPSILON)
        normed[rows, :] = (floats * scale).astype(jnp.bfloat16)
        return carry

    lax.fori_loop(0, toks // ROWS, normalize, 0)
    logits[...] = dot(normed[...], keys[...])

    slot_level = pick(iota((1, slots), 1), reach_width, [reach[0, b] for b in range(reach.shape[1])])
    for b in range(slots // 128):
        cols = slice(b * 128, (b + 1) * 128)
        allowed = iota((toks, 128), 0) // BLOCK <= slot_level[:, cols]
        masked = jnp.where(allowed, logits[:, cols], -jnp.inf)
        exponent = jnp.exp(masked - jnp.max(masked, axis=0, keepdims=True))
        weights[:, cols] = (exponent / jnp.sum(exponent, axis=0, keepdims=True)).astype(jnp.bfloat16)
    slot_in[...] = lax.dot_general(
        weights[...], normed[...], (((0,), (0,)), ((), ())), preferred_element_type=jnp.float32
    ).astype(jnp.bfloat16)

    taken = [counts[0, e] for e in range(experts)]
    starts = []
    total = jnp.int32(0)
    for e in range(experts):
        starts.append(total)
        total = total + taken[e]

    pl.semaphore_wait(barrier, n_exp + 1)

    group = n_exp * cap
    mine = pl.ds(pl.multiple_of(me * cap, cap), cap)

    def to_expert(j, o):
        peer = lax.rem(me + o, n_exp)
        theirs = pl.ds(pl.multiple_of(peer * cap, cap), cap)
        return pltpu.make_async_remote_copy(
            src_ref=send.at[j, theirs],
            dst_ref=recv.at[j, mine],
            send_sem=send_in.at[j, o],
            recv_sem=recv_in.at[j, o],
            device_id=(ctx, peer),
            device_id_type=MESH,
        )

    def to_home(j, o):
        peer = lax.rem(me + o, n_exp)
        theirs = pl.ds(pl.multiple_of(peer * cap, cap), cap)
        there = pl.ds(pl.multiple_of((me * local + j) * cap, cap), cap)
        return pltpu.make_async_remote_copy(
            src_ref=prod.at[j, theirs],
            dst_ref=ret.at[there],
            send_sem=send_out.at[j, o],
            recv_sem=recv_out.at[j, o],
            device_id=(ctx, peer),
            device_id_type=MESH,
        )

    for j in range(local):
        chosen = [d * local + j for d in range(n_exp)]
        row = iota((group, 1), 0)
        shift = pick(row, cap, [starts[e] - d * cap for d, e in enumerate(chosen)])
        limit = pick(row, cap, [taken[e] + d * cap for d, e in enumerate(chosen)])
        source = jnp.where(row < limit, row + shift, -1)
        hot = jnp.where(iota((group, slots), 1) == source, 1.0, 0.0).astype(jnp.bfloat16)
        send[j] = dot(hot, slot_in[...]).astype(jnp.bfloat16)
        for o in range(1, n_exp):
            to_expert(j, o).start()
        recv[j, mine, :] = send[j, mine, :]

    column = iota((1, experts * cap), 1)
    shift = pick(column, cap, [starts[e] - e * cap for e in range(experts)])
    limit = pick(column, cap, [taken[e] + e * cap for e in range(experts)])
    source = jnp.where(column < limit, column + shift, -1)
    has_prior = window > 0

    def ready(i, carry):
        rows = pl.ds(pl.multiple_of(i * ROWS, ROWS), ROWS)
        slot = iota((ROWS, experts * cap), 0) + i * ROWS
        place[rows, :] = jnp.where(slot == source, 1.0, 0.0).astype(jnp.bfloat16)
        return carry

    lax.fori_loop(0, slots // ROWS, ready, 0)

    def mixing(i, carry):
        rows = pl.ds(pl.multiple_of(i * ROWS, ROWS), ROWS)
        level = (iota((ROWS, slots), 0) + i * ROWS) // BLOCK
        allowed = slot_level <= level
        usable = jnp.logical_or(allowed, has_prior)
        masked = jnp.where(usable, logits[rows, :], -jnp.inf)
        every = jnp.exp(masked - jnp.max(masked, axis=1, keepdims=True))
        own = jnp.where(allowed, every, 0.0)
        prior = jnp.where(has_prior, every, 0.0)
        denominator = jnp.sum(own + prior, axis=1, keepdims=True)
        mix_w[rows, :slots] = (own / denominator).astype(jnp.bfloat16)
        mix_w[rows, slots:] = (prior / denominator).astype(jnp.bfloat16)
        return carry

    lax.fori_loop(0, toks // ROWS, mixing, 0)

    tile = min(512, hidden)

    for j in range(local):
        loads[2 * j].wait()
        loads[2 * j + 1].wait()
        for o in range(1, n_exp):
            to_expert(j, o).wait_recv()
        total_out = None
        for t in range(hidden // tile):
            cols = slice(t * tile, (t + 1) * tile)
            active = jax.nn.gelu(dot(recv[j], first_v[j, :, cols]), approximate=True)
            term = dot(active.astype(jnp.bfloat16), second_v[j, cols, :])
            total_out = term if total_out is None else total_out + term
        prod[j] = total_out.astype(jnp.bfloat16)
        for o in range(1, n_exp):
            to_home(j, o).start()
        here = pl.ds(pl.multiple_of((me * local + j) * cap, cap), cap)
        ret[here, :] = prod[j, mine, :]

    for j in range(local):
        for o in range(1, n_exp):
            to_home(j, o).wait_recv()

    piece = slots // PIECES

    def to_next(p):
        return pltpu.make_async_remote_copy(
            src_ref=mix_v.at[pl.ds(p * piece, piece)],
            dst_ref=mix_v.at[pl.ds(slots + p * piece, piece)],
            send_sem=send_prior.at[p],
            recv_sem=recv_prior.at[p],
            device_id=(after // n_exp, lax.rem(after, n_exp)),
            device_id_type=MESH,
        )

    for p in range(PIECES):
        rows = slice(p * piece, (p + 1) * piece)
        mix_v[rows, :] = dot(place[rows, :], ret[...]).astype(jnp.bfloat16)

        @pl.when(window < windows - 1)
        def _():
            to_next(p).start()

    @pl.when(window == 0)
    def _():
        mix_v[slots:, :] = jnp.zeros((slots, width), jnp.bfloat16)

    @pl.when(window > 0)
    def _():
        for p in range(PIECES):
            to_next(p).wait_recv()

    out[...] = dot(mix_w[...], mix_v[...]).astype(jnp.bfloat16)

    @pl.when(window < windows - 1)
    def _():
        for p in range(PIECES):
            to_next(p).wait_send()

    for j in range(local):
        for o in range(1, n_exp):
            to_expert(j, o).wait_send()
            to_home(j, o).wait_send()


def layer(n_ctx, n_exp, tokens, slot_keys, expert_in, expert_out, slot_counts, slot_reach):
    toks, width = tokens.shape
    slots = slot_keys.shape[1]
    local = expert_in.shape[0]
    experts = slot_counts.shape[1]
    cap = 2 * slots // experts
    bf16, f32 = jnp.bfloat16, jnp.float32
    in_vmem = pl.BlockSpec(memory_space=pltpu.VMEM)
    in_smem = pl.BlockSpec(memory_space=pltpu.SMEM)
    in_any = pl.BlockSpec(memory_space=pl.ANY)
    dma = pltpu.SemaphoreType.DMA
    return pl.pallas_call(
        functools.partial(kernel, n_ctx, n_exp),
        out_shape=jax.ShapeDtypeStruct((toks, width), bf16),
        in_specs=[in_smem, in_smem, in_vmem, in_vmem, in_any, in_any],
        out_specs=in_vmem,
        scratch_shapes=[
            pltpu.VMEM(expert_in.shape, bf16),
            pltpu.VMEM(expert_out.shape, bf16),
            pltpu.VMEM((toks, width), bf16),
            pltpu.VMEM((toks, slots), f32),
            pltpu.VMEM((toks, slots), bf16),
            pltpu.VMEM((slots, width), bf16),
            pltpu.VMEM((local, n_exp * cap, width), bf16),
            pltpu.VMEM((local, n_exp * cap, width), bf16),
            pltpu.VMEM((local, n_exp * cap, width), bf16),
            pltpu.VMEM((experts * cap, width), bf16),
            pltpu.VMEM((slots, experts * cap), bf16),
            pltpu.VMEM((toks, 2 * slots), bf16),
            pltpu.VMEM((2 * slots, width), bf16),
            dma((local, 2)),
            dma((local, n_exp)),
            dma((local, n_exp)),
            dma((local, n_exp)),
            dma((local, n_exp)),
            dma((PIECES,)),
            dma((PIECES,)),
        ],
        compiler_params=pltpu.CompilerParams(
            collective_id=0, has_side_effects=True, vmem_limit_bytes=67043328
        ),
    )(slot_counts, slot_reach, tokens, slot_keys, expert_in, expert_out)


def solution(mesh):
    placed = (
        P(("ctx", "exp"), None),
        P(),
        P("exp", None, None),
        P("exp", None, None),
        P(("ctx", "exp"), None),
        P(("ctx", "exp"), None),
    )
    body = functools.partial(layer, mesh.shape["ctx"], mesh.shape["exp"])
    return jax.shard_map(
        body, mesh=mesh, in_specs=placed, out_specs=P(("ctx", "exp"), None), check_vma=False
    )
```

time: 124 us -> 82.6 us (0.67)
  Pallas kernels: 0 us -> 79.7 us
  waiting for transfers between devices: 49.6 us -> 0 us
  blocking collectives: 27.4 us -> 0 us
  matrix products: 24.3 us -> 0 us
  local copies, waits for them, and re-layouts: 10.8 us -> 2.26 us
  other arithmetic: 6.09 us -> 0 us
  starting transfers between devices: 5.53 us -> 0 us
    pallas_call x0 -> x1, Pallas kernels: none -> 79.7 us  [layer(): pl.pallas_call(functools.partial(kernel, n_ctx, n_exp), out_shape=jax.Sha...]
    all_to_all x1 -> x0, blocking collectives: 27.4 us -> none  [local(): lax.all_to_all(outgoing, 'exp', split_axis=0, concat_axis=1, tiled=True)]
    ppermute x1 -> x0, waiting for transfers between devices: 25.4 us -> none  [passed_along(): return lax.ppermute(block, axis, route)]
    dot_general x6 -> x0, matrix products: 24.3 us -> none  [the longest x1 10 us: local_experts(): jnp.einsum('epcd,edh->epch', received, w_first, preferred_element_type=jn...]
    all_to_all x1 -> x0, waiting for transfers between devices: 24.1 us -> none  [local(): lax.all_to_all(produced, 'exp', split_axis=1, concat_axis=0, tiled=True)]
    gather x2 -> x0, local copies, waits for them, and re-layouts: 8.12 us -> none  [the longest x1 5.35 us: dispatch_window(): jnp.take(slot_inputs, source, axis=0)]
    all_to_all x1 -> x0, starting transfers between devices: 3.61 us -> none  [local(): lax.all_to_all(produced, 'exp', split_axis=1, concat_axis=0, tiled=True)]
    select_n x6 -> x0, other arithmetic: 3.29 us -> none  [the longest x1 1.78 us: dispatch_window(): jnp.where(is_live[:, None], jnp.take(slot_inputs, source, axis=0), jnp.ze...]
  transfers between devices with their start and end apart: 2 -> 0, of which waited for: 2 -> 0; matrix products, arithmetic and copies ran while one was open for 1% -> 0% of each run, Pallas kernels for 0% -> 0%
where the time goes in v1:
time: 82.6 us; the launch traced here: 81.9 us
  Pallas kernels  79.7 us (96%)
  local copies, waits for them, and re-layouts  2.26 us (3%)
    pallas_call x1, Pallas kernels, layer(): pl.pallas_call(functools.partial(kernel, n_ctx, n_exp), out_shape=jax.Sha...  79.7 us
    unnamed x1, local copies, waits for them, and re-layouts  2.26 us

profile of v1, /device:TPU:25, one launch (start us, length us, event | category | flops | bytes accessed | tf_op | source)
XLA Modules:
  0.0 81.9 jit_solution(417644419496468193)
XLA Ops:
  0.0 79.7 %shard_map.64 = bf16[512,1024]{1,0:T(8,128)(2,1)} custom-call(s32[1,16]{1,0:T(1,128)} %counts.1, s32[1,8]{1,0:T(1,128)} %reach.1, bf16[512,1024]{1,0:T(8,128)(2,1)} %tokens.1, bf16[1024,512]{1,0:T(8,128)(2,1)} %keys.1, bf16[4,1024,2048]{2,1,0:T(8,128)(2,1)} %first.1, bf16[4,2048,1024]{2,1,0:T(8,128)(2,1)} %second.1), custom_call_target="tpu_custom_call" | custom-call | tf_op jit(solution)/shard_map/pallas_call | solution.py:243
  79.7 2.3 %copy.8 = bf16[512,1024]{1,0:T(8,128)(2,1)} copy(bf16[512,1024]{1,0:T(8,128)(2,1)} %shard_map.64) | data formatting | bytes 2097152

commit v2 on v1

--- a/solution.py
+++ b/solution.py
@@ -31,7 +31,7 @@
 
 def kernel(
     n_ctx, n_exp, counts, reach, tokens, keys, first, second, out,
-    first_v, second_v, normed, logits, weights, slot_in, send, recv, prod, ret, place, mix_w, mix_v,
+    first_v, second_v, normed, logits, weights, slot_in, send, recv, prod, ret, place, mix_w, mix_v, summed,
     weight_sem, send_in, recv_in, send_out, recv_out, send_prior, recv_prior,
 ):
     toks, width = tokens.shape
@@ -211,12 +211,22 @@
     def _():
         mix_v[slots:, :] = jnp.zeros((slots, width), jnp.bfloat16)
 
-    @pl.when(window > 0)
-    def _():
-        for p in range(PIECES):
+    def mix(first_col, last_col):
+        cols = slice(first_col, last_col)
+        return dot(mix_w[:, cols], mix_v[cols, :])
+
+    def arrived(p):
+        @pl.when(window > 0)
+        def _():
             to_next(p).wait_recv()
 
-    out[...] = dot(mix_w[...], mix_v[...]).astype(jnp.bfloat16)
+    summed[...] = mix(0, slots)
+    late = slots + (PIECES - 1) * piece
+    for p in range(PIECES - 1):
+        arrived(p)
+    summed[...] += mix(slots, late)
+    arrived(PIECES - 1)
+    out[...] = (summed[...] + mix(late, 2 * slots)).astype(jnp.bfloat16)
 
     @pl.when(window < windows - 1)
     def _():
@@ -242,7 +252,7 @@
     dma = pltpu.SemaphoreType.DMA
     return pl.pallas_call(
         functools.partial(kernel, n_ctx, n_exp),
-        out_shape=jax.ShapeDtypeStruct((toks, width), bf16),
+        out_shape=pltpu.VMEM((toks, width), bf16),
         in_specs=[in_smem, in_smem, in_vmem, in_vmem, in_any, in_any],
         out_specs=in_vmem,
         scratch_shapes=[
@@ -259,6 +269,7 @@
             pltpu.VMEM((slots, experts * cap), bf16),
             pltpu.VMEM((toks, 2 * slots), bf16),
             pltpu.VMEM((2 * slots, width), bf16),
+            pltpu.VMEM((toks, width), f32),
             dma((local, 2)),
             dma((local, n_exp)),
             dma((local, n_exp)),
@@ -268,7 +279,7 @@
             dma((PIECES,)),
         ],
         compiler_params=pltpu.CompilerParams(
-            collective_id=0, has_side_effects=True, vmem_limit_bytes=67043328
+            collective_id=0, has_side_effects=True, vmem_limit_bytes=60*2**20
         ),
     )(slot_counts, slot_reach, tokens, slot_keys, expert_in, expert_out)
 

time: 82.6 us -> 79.5 us (0.962)
  Pallas kernels: 79.7 us -> 77.8 us
  local copies, waits for them, and re-layouts: 2.26 us -> 0.97 us
    pallas_call x1, Pallas kernels: 79.7 us -> 77.8 us  [layer(): pl.pallas_call(functools.partial(kernel, n_ctx, n_exp), out_shape=pltpu.V...]
    unnamed x1, local copies, waits for them, and re-layouts: 2.26 us -> 0.97 us
where the time goes in v2:
time: 79.5 us; the launch traced here: 78.8 us
  Pallas kernels  77.8 us (98%)
  local copies, waits for them, and re-layouts  0.97 us (1%)
    pallas_call x1, Pallas kernels, layer(): pl.pallas_call(functools.partial(kernel, n_ctx, n_exp), out_shape=pltpu.V...  77.8 us

profile of v2, /device:TPU:25, one launch (start us, length us, event | category | flops | bytes accessed | tf_op | source)
XLA Modules:
  0.0 78.8 jit_solution(6841963103099063055)
XLA Ops:
  0.0 77.8 %shard_map.64 = bf16[512,1024]{1,0:T(8,128)(2,1)S(1)} custom-call(s32[1,16]{1,0:T(1,128)} %counts.1, s32[1,8]{1,0:T(1,128)} %reach.1, bf16[512,1024]{1,0:T(8,128)(2,1)} %tokens.1, bf16[1024,512]{1,0:T(8,128)(2,1)} %keys.1, bf16[4,1024,2048]{2,1,0:T(8,128)(2,1)} %first.1, bf16[4,2048,1024]{2,1,0:T(8,128)(2,1)} %second.1), custom_call_target="tpu_custom_call" | custom-call | tf_op jit(solution)/shard_map/pallas_call | solution.py:253
  77.9 1.0 %copy.8 = bf16[512,1024]{1,0:T(8,128)(2,1)} copy(bf16[512,1024]{1,0:T(8,128)(2,1)S(1)} %shard_map.64) | data formatting | bytes 2097152
